TPU v7x, 256 devices: a whole 4x4x8 slice. The times are simulated.
256 devices in a mesh: space: 32 (over y, z), spec: 8 (over x, core).
Axes of the slice: x: 4, y: 4, z: 8, core: 2. Of those that a mesh axis runs over, the one named last changes fastest.
Arguments:
- spectra: float32 [1296, 32768], P('spec', 'space'), may hold values from 0.1 to 2
- wet_mask: int32 [32768], P('space'), may hold values 0 or 1
- depth_class: int32 [32768], P('space'), may hold values from 0 to 31
- cg_table: float32 [36, 32], replicated, may hold values from 0.3 to 1
- neighbour: int32 [8, 32768], P(None, 'space'), may hold values from 0 to 3071, as said below
- edge_weight: float32 [8, 32768], P(None, 'space'), may hold values from 0.02 to 0.11
- edge_angle: float32 [8, 32768], P(None, 'space'), may hold values from -3.140625 to 3.140625
- send_list: int32 [32, 32, 64], P('space'), may hold values from 0 to 1023, as said below
- friction: float32 [32768], P('space'), may hold values from 0.2 to 1.5
- wind_dir: float32 [32768], P('space'), may hold values from -3.140625 to 3.140625
Outputs:
- spectra_next: float32 [1296, 32768], P('spec', 'space')
- energy: float32 [32768], P(('space', 'spec'))
Inputs may be any that keep to these rules, and one draw needn't show every extreme that they name: `send_list`: block s sends only to blocks (s + 1), (s - 1), (s + 2), (s - 2) and (s + 16), all modulo 32; entries of any other pair, and entries at or past a pair's used count, are 0. The pair from each block s to block (s + 1) % 32 uses all 64 slots and its slot 0 holds node 1023. `neighbour`: A ghost entry 1024 + p * 64 + g has p among the blocks that send to the node's block and g below the count that block p uses towards it; an unused slot holds the node's own local index. Node 0 of every block b has slot 0 at ghost slot 63 from block (b - 1) % 32.
All inputs are finite; a program needn't handle non-finite values. No bound on the sum of `wet_mask` on one device may be relied on, other than what follows from the above.
Results may differ from a plain program's by a relative error of at most 0.000067.
Values sent between devices are 32-bit elements; how exact they have to be, the bound alone decides.
No kernel may reach another device: no remote copies, remote signals or barrier semaphores. Data moves between devices by JAX's collectives and lax.ppermute only.
A program may use at most 64 MiB of HBM per device.

v0:
```python
import math
import jax
import jax.numpy as jnp
from jax import lax
from jax.sharding import PartitionSpec as P

NDIR = 36
NFREQ = 36
NCLASS = 32


def spectral_constants():
    level_index = jnp.arange(NFREQ, dtype=jnp.float32)
    frequency = 0.04 * jnp.exp(level_index * jnp.float32(math.log(1.1)))
    spread = 0.1 * frequency
    band_weight = spread / (NDIR * jnp.sum(spread))
    direction_angle = jnp.arange(NDIR, dtype=jnp.float32) * jnp.float32(2.0 * math.pi / NDIR)
    return (frequency, band_weight, jnp.cos(direction_angle), jnp.sin(direction_angle))


def point_source(values, energy, moment, freq_col, cos_col, sin_col, friction_row, dir_row):
    top_freq = 0.04 * jnp.exp(jnp.float32(NFREQ - 1) * jnp.float32(math.log(1.1)))
    mean_freq = (moment + 4e-08) / (energy + 1e-06)
    steepness = energy * (mean_freq / 0.8) ** 4
    dissipation = (steepness**2)[None, :] * freq_col[:, None] / mean_freq[None, :]
    drive = (
        cos_col[:, None] * jnp.cos(dir_row)[None, :] + sin_col[:, None] * jnp.sin(dir_row)[None, :]
    )
    relative = freq_col / top_freq
    wind_input = 0.5 * jnp.maximum(
        4.0 * friction_row[None, :] * relative[:, None] * drive - 1.0, 0.0
    )
    return values * jnp.exp(0.25 * (wind_input - dissipation))


def per_device(
    spectra,
    wet_mask,
    depth_class,
    cg_table,
    neighbour,
    edge_weight,
    edge_angle,
    send_list,
    friction,
    wind_dir,
):
    comp_count, node_count = spectra.shape
    spec_count = lax.axis_size("spec")
    slot_count = neighbour.shape[0]
    frequency, band_weight, dir_cosine, dir_sine = spectral_constants()
    comp_range = lax.axis_index("spec") * comp_count + jnp.arange(comp_count, dtype=jnp.int32)
    freq_index = comp_range // NDIR
    dir_index = comp_range % NDIR
    cos_col = dir_cosine[dir_index]
    sin_col = dir_sine[dir_index]
    wet_float = wet_mask.astype(jnp.float32)
    masked = spectra * wet_float[None, :]
    outgoing = jnp.take(masked, send_list[0].reshape(-1), axis=1)
    ghost_values = lax.all_to_all(outgoing, "space", split_axis=1, concat_axis=1, tiled=True)
    class_hits = (jnp.arange(NCLASS, dtype=jnp.int32)[:, None] == depth_class[None, :]).astype(
        jnp.float32
    )
    group_speed = jnp.dot(
        cg_table[freq_index],
        class_hits,
        precision=lax.Precision.HIGHEST,
        preferred_element_type=jnp.float32,
    )
    accumulated = jnp.zeros_like(masked)
    extended = jnp.concatenate([masked, ghost_values], axis=1)
    gathered_all = jnp.take(extended, neighbour.reshape(-1), axis=1)
    for slot_index in range(slot_count):
        gathered = gathered_all[:, slot_index * node_count : (slot_index + 1) * node_count]
        alignment = (
            cos_col[:, None] * jnp.cos(edge_angle[slot_index])[None, :]
            + sin_col[:, None] * jnp.sin(edge_angle[slot_index])[None, :]
        )
        accumulated = accumulated + group_speed * edge_weight[slot_index][None, :] * jnp.maximum(
            alignment, 0.0
        ) * (gathered - masked)
    advected = (masked + accumulated) * wet_float[None, :]
    point_count = node_count // spec_count
    offset = lax.axis_index("spec") * point_count
    blocked = advected.reshape(comp_count, spec_count, point_count)
    gathered_points = lax.all_to_all(
        blocked, "spec", split_axis=1, concat_axis=0, tiled=True
    ).reshape(comp_count * spec_count, point_count)
    full_range = jnp.arange(comp_count * spec_count, dtype=jnp.int32)
    full_freq = full_range // NDIR
    full_dir = full_range % NDIR
    freq_col = frequency[full_freq]
    weight_col = band_weight[full_freq]
    energy = jnp.sum(gathered_points * weight_col[:, None], axis=0)
    moment = jnp.sum(gathered_points * (weight_col * freq_col)[:, None], axis=0)
    friction_part = lax.dynamic_slice_in_dim(friction, offset, point_count)
    wind_part = lax.dynamic_slice_in_dim(wind_dir, offset, point_count)
    updated = point_source(
        gathered_points,
        energy,
        moment,
        freq_col,
        dir_cosine[full_dir],
        dir_sine[full_dir],
        friction_part,
        wind_part,
    )
    returned = lax.all_to_all(
        updated.reshape(comp_count * spec_count, 1, point_count),
        "spec",
        split_axis=0,
        concat_axis=1,
        tiled=True,
    )
    return (returned.reshape(comp_count, node_count), energy)


def solution(mesh):
    placed = (
        P("spec", "space"),
        P("space"),
        P("space"),
        P(),
        P(None, "space"),
        P(None, "space"),
        P(None, "space"),
        P("space", None, None),
        P("space"),
        P("space"),
    )
    return jax.shard_map(
        per_device,
        mesh=mesh,
        in_specs=placed,
        out_specs=(P("spec", "space"), P(("space", "spec"))),
        check_vma=False,
    )
```

profile of v0, /device:TPU:1, one launch (start us, length us, event | category | flops | bytes accessed | tf_op | source)
XLA Modules:
  0.0 211.6 jit_solution(6362153186703250153)
XLA Ops:
  0.6 0.8 reshape_squeeze.6
  1.4 0.7 compare_and_fusion.1
  2.2 0.7 convert_element_type.4
  2.8 1.2 broadcast_multiply_fusion
  4.0 0.3 copy.29
  4.4 6.6 %gather_fusion.3 = f32[2048,162]{1,0:T(8,128)S(1)} fusion(f32[162,1024]{0,1:T(8,128)S(1)} %copy.29, s32[2048]{0:T(1024)S(1)} %broadcast_clamp_fusion.1), kind=kCustom, calls=%fused_computation.3 | custom fusion | bytes 2662400 | tf_op jit(solution)/shard_map/jit(_take)/gather | solution.py:59
  11.0 1.7 broadcast_select_fusion
  12.7 12.2 %all-to-all-start = ((f32[162,32,64]{0,2,1:T(8,128)}), f32[162,32,64]{0,2,1:T(8,128)S(1)}, u32[]{:S(2)}, u32[]{:S(2)}) async-start(f32[162,32,64]{0,2,1:T(8,128)} %broadcast_select_fusion), calls=%async_computation | async-start | bytes 4194304 | tf_op jit(solution)/shard_map/all_to_all | solution.py:60
  26.8 0.6 fusion.27
  28.1 0.7 fusion.36
  28.8 0.7 fusion.35
  29.6 0.7 fusion.34
  30.3 0.7 fusion.33
  31.0 0.1 compare_reduce_fusion
  31.1 0.1 compare_reduce_fusion.1
  31.2 0.1 compare_reduce_fusion.2
  31.2 0.1 compare_reduce_fusion.3
  31.3 0.1 compare_reduce_fusion.4
  31.4 0.1 compare_reduce_fusion.5
  31.5 0.1 compare_reduce_fusion.6
  31.5 0.1 compare_reduce_fusion.7
  31.6 0.1 compare_reduce_fusion.8
  31.7 0.1 compare_reduce_fusion.9
  31.9 0.1 compare_reduce_fusion.12
  32.1 0.1 compare_reduce_fusion.15
  32.2 0.1 compare_reduce_fusion.17
  32.4 0.1 compare_reduce_fusion.20
  32.7 0.1 compare_reduce_fusion.23
  33.0 0.7 fusion.32
  33.7 0.7 fusion.31
  34.5 1.6 gather_fusion.2
  36.1 1.6 gather_fusion.1
  37.6 0.7 fusion.30
  38.4 0.1 copy.27
  38.5 0.7 gather_fusion
  39.2 0.8 dynamic-slice_cosine_fusion
  40.0 4.5 %fusion.18 = f32[1296]{0:T(1024)S(1)} fusion(f32[]{:T(128)} %bitcast.173, f32[]{:T(128)} %bitcast.174, f32[]{:T(128)} %bitcast.175, f32[]{:T(128)} %bitcast.176, f32[]{:T(128)} %bitcast.177, f32[]{:T(128)} %bitcast.179, f32[]{:T(128)} %bitcast.178), kind=kLoop, calls=%fused_computation.142 | loop fusion | flops 29808 | bytes 5212 | tf_op jit(solution)/shard_map/gather | solution.py:93
  44.5 4.3 %fusion.19 = f32[1296]{0:T(1024)S(1)} fusion(f32[]{:T(128)} %bitcast.64, f32[]{:T(128)} %bitcast.65, f32[]{:T(128)} %bitcast.66, f32[]{:T(128)} %bitcast.67, f32[]{:T(128)} %bitcast.68, f32[]{:T(128)} %bitcast.70, f32[]{:T(128)} %bitcast.69), kind=kLoop, calls=%fused_computation.143 | loop fusion | flops 29808 | bytes 5212 | tf_op jit(solution)/shard_map/gather | solution.py:92
  48.8 4.3 %fusion.20 = f32[1296]{0:T(1024)S(1)} fusion(f32[]{:T(128)} %bitcast.136, f32[]{:T(128)} %bitcast.137, f32[]{:T(128)} %bitcast.138, f32[]{:T(128)} %bitcast.139, f32[]{:T(128)} %bitcast.140, f32[]{:T(128)} %bitcast.142, f32[]{:T(128)} %bitcast.141), kind=kLoop, calls=%fused_computation.144 | loop fusion | flops 27216 | bytes 5212 | tf_op jit(solution)/shard_map/gather | solution.py:104
  53.2 17.8 %select_select_fusion = f32[1296]{0:T(1024)S(1)} fusion(pred[1296]{0:T(1024)(128)(4,1)S(1)} %compare_reduce_fusion.29, pred[1296]{0:T(1024)(128)(4,1)S(1)} %compare_reduce_fusion.30, pred[1296]{0:T(1024)(128)(4,1)S(1)} %compare_reduce_fusion.31, pred[1296]{0:T(1024)(128)(4,1)S(1)} %compare_reduce_fusion.32, pred[1296]{0:T(1024)(128)(4,1)S(1)} %compare_reduce_fusion.33, ...), kind=kLoop, calls=%fused_computation.136 | loop fusion | flops 37584 | bytes 48068 | tf_op jit(solution)/shard_map/gather | solution.py:93
  71.1 18.0 %broadcast_multiply_fusion.1 = (f32[1296]{0:T(1024)S(1)}, f32[1296]{0:T(1024)S(1)}) fusion(pred[1296]{0:T(1024)(128)(4,1)S(1)} %compare_reduce_fusion.29, pred[1296]{0:T(1024)(128)(4,1)S(1)} %compare_reduce_fusion.30, pred[1296]{0:T(1024)(128)(4,1)S(1)} %compare_reduce_fusion.31, pred[1296]{0:T(1024)(128)(4,1)S(1)} %compare_reduce_fusion.32, ...), kind=kLoop, calls=%fused_computation.149 | loop fusion | flops 38880 | bytes 53252 | tf_op jit(solution)/shard_map/div | solution.py:29
  89.1 1.0 slice_cosine_fusion.7
  90.1 1.3 copy-done.1
  91.5 2.1 pad_maximum_fusion
  93.5 31.4 %gather_fusion.4 = f32[8192,162]{1,0:T(8,128)} fusion(f32[162,3072]{0,1:T(8,128)S(1)} %pad_maximum_fusion, s32[8192]{0:T(1024)S(1)} %broadcast_clamp_fusion), kind=kCustom, calls=%fused_computation.4 | custom fusion | bytes 10649600 | tf_op jit(solution)/shard_map/jit(_take)/gather | solution.py:72
  124.9 8.4 %copy.30 = f32[8192,162]{0,1:T(8,128)} copy(f32[8192,162]{1,0:T(8,128)} %gather_fusion.4) | data formatting | bytes 10616832 | tf_op jit(solution)/shard_map/jit(_take)/gather | solution.py:72
  133.3 3.1 %select_bitcast_fusion = f32[162,8192]{1,0:T(8,128)S(1)} fusion(f32[8192,162]{0,1:T(8,128)} %copy.30, pred[8192]{0:T(1024)(128)(4,1)S(1)} %compare_and_fusion), kind=kLoop, calls=%fused_computation.5 | loop fusion | flops 1327104 | bytes 10625024 | tf_op jit(solution)/shard_map/jit(_take)/select_n | solution.py:72
  136.4 2.4 %fusion.3 = f32[162,1024]{1,0:T(8,128)S(1)} fusion(f32[162,8192]{1,0:T(8,128)S(1)} %select_bitcast_fusion, f32[162,32]{1,0:T(8,128)S(1)} %gather_fusion, f32[1024]{0:T(1024)S(1)} %bitcast.243, f32[1024]{0:T(1024)S(1)} %bitcast.249, f32[1024]{0:T(1024)S(1)} %bitcast.233, f32[1024]{0:T(1024)S(1)} %bitcast.242, f32[1024]{0:T(1024)S(1)} %bitcast.250, ...), kind=kOutput, calls=%fused_computation.12 | convolution fusion | flops 76009472 | bytes 6764048 | tf_op jit(solution)/shard_map/dot_general | solution.py:64
  138.8 0.1 copy.39
  139.0 1.0 copy.31
  140.0 5.2 %all-to-all-start.1 = ((f32[162,8,128]{2,0,1:T(8,128)}), f32[162,8,128]{2,0,1:T(8,128)S(1)}, u32[]{:S(2)}, u32[]{:S(2)}) async-start(f32[162,8,128]{2,0,1:T(8,128)} %copy.31), calls=%async_computation.1 | async-start | bytes 1376256 | tf_op jit(solution)/shard_map/all_to_all | solution.py:86
  145.3 0.1 mul.694
  145.4 0.1 gather.43
  145.5 4.6 %fusion.21 = f32[1296]{0:T(1024)S(1)} fusion(f32[]{:T(128)} %bitcast.100, f32[]{:T(128)} %bitcast.101, f32[]{:T(128)} %bitcast.102, f32[]{:T(128)} %bitcast.103, f32[]{:T(128)} %bitcast.104, f32[]{:T(128)} %bitcast.106, f32[]{:T(128)} %bitcast.105), kind=kLoop, calls=%fused_computation.145 | loop fusion | flops 27216 | bytes 5212 | tf_op jit(solution)/shard_map/gather | solution.py:103
  150.0 0.7 fusion.29
  150.8 18.1 %select_select_fusion.1 = f32[1296]{0:T(1024)S(1)} fusion(pred[1296]{0:T(1024)(128)(4,1)S(1)} %compare_reduce_fusion, pred[1296]{0:T(1024)(128)(4,1)S(1)} %compare_reduce_fusion.1, pred[1296]{0:T(1024)(128)(4,1)S(1)} %compare_reduce_fusion.2, pred[1296]{0:T(1024)(128)(4,1)S(1)} %compare_reduce_fusion.3, pred[1296]{0:T(1024)(128)(4,1)S(1)} %compare_reduce_fusion.4, ...), kind=kLoop, calls=%fused_computation.137 | loop fusion | flops 37584 | bytes 48068 | tf_op jit(solution)/shard_map/gather | solution.py:104
  168.9 18.2 %select_select_fusion.2 = f32[1296]{0:T(1024)S(1)} fusion(pred[1296]{0:T(1024)(128)(4,1)S(1)} %compare_reduce_fusion, pred[1296]{0:T(1024)(128)(4,1)S(1)} %compare_reduce_fusion.1, pred[1296]{0:T(1024)(128)(4,1)S(1)} %compare_reduce_fusion.2, pred[1296]{0:T(1024)(128)(4,1)S(1)} %compare_reduce_fusion.3, pred[1296]{0:T(1024)(128)(4,1)S(1)} %compare_reduce_fusion.4, ...), kind=kLoop, calls=%fused_computation.138 | loop fusion | flops 37584 | bytes 48068 | tf_op jit(solution)/shard_map/gather | solution.py:103
  187.2 0.4 multiply_reduce_fusion
  187.6 1.1 exponential_multiply_fusion
  188.7 15.6 %all_to_all.39 = f32[1296,1,128]{2,1,0:T(1,128)S(1)} all-to-all(f32[1296,1,128]{2,1,0:T(1,128)S(1)} %bitcast.218), channel_id=1, replica_groups=mesh['space'=32,'spec'=8] {'spec'}, dimensions={0} | all-to-all | bytes 1327104 | tf_op jit(solution)/shard_map/all_to_all | solution.py:108
  204.4 0.5 broadcast.1224
  204.9 5.5 %reduce.129 = f32[1296,128]{1,0:T(8,128)S(1)} reduce(f32[1296,1,128]{2,1,0:T(1,128)S(1)} %all_to_all.39, f32[]{:T(128)} %broadcast.1224), dimensions={1}, to_apply=%all_to_all.33.reduce_sub_computation.3 | reduce | bytes 1327108 | tf_op jit(solution)/shard_map/all_to_all | solution.py:108
  210.4 0.1 copy.46
  210.6 1.0 copy.40
  (82 shorter events, 3.3 us)
Async XLA Ops:
  4.3 6.7 %copy-start = (f32[162,1024]{0,1:T(8,128)}, f32[162,1024]{0,1:T(8,128)S(1)}, u32[]{:S(2)}) copy-start(f32[162,1024]{0,1:T(8,128)S(1)} %copy.29) | copy-start | bytes 1990660
  12.7 25.6 %copy-start.3 = (s32[8,1024]{1,0:T(8,128)S(1)}, s32[8,1024]{1,0:T(8,128)}, u32[]{:S(2)}) copy-start(s32[8,1024]{1,0:T(8,128)} %param.14) | copy-start | bytes 98308
  12.7 25.7 %copy-start.6 = (f32[36,32]{0,1:T(8,128)S(1)}, f32[36,32]{0,1:T(8,128)}, u32[]{:S(2)}) copy-start(f32[36,32]{0,1:T(8,128)} %param.13) | copy-start | bytes 13828
  12.7 40.5 %copy-start.5 = (f32[8,1024]{1,0:T(8,128)S(1)}, f32[8,1024]{1,0:T(8,128)}, u32[]{:S(2)}) copy-start(f32[8,1024]{1,0:T(8,128)} %param.15) | copy-start | bytes 98308
  12.7 76.3 %copy-start.4 = (f32[8,1024]{1,0:T(8,128)S(1)}, f32[8,1024]{1,0:T(8,128)}, u32[]{:S(2)}) copy-start(f32[8,1024]{1,0:T(8,128)} %param.16) | copy-start | bytes 98308
  12.7 77.4 %all-to-all-start = ((f32[162,32,64]{0,2,1:T(8,128)}), f32[162,32,64]{0,2,1:T(8,128)S(1)}, u32[]{:S(2)}, u32[]{:S(2)}) async-start(f32[162,32,64]{0,2,1:T(8,128)} %broadcast_select_fusion), calls=%async_computation | async-start | bytes 4194304 | tf_op jit(solution)/shard_map/all_to_all | solution.py:60
  90.1 1.4 copy-start.1
  133.3 3.1 %copy-start.2 = (f32[162,1024]{1,0:T(8,128)S(1)}, f32[162,1024]{1,0:T(8,128)}, u32[]{:S(2)}) copy-start(f32[162,1024]{1,0:T(8,128)} %param.10) | copy-start | bytes 1990660
  133.3 3.1 %copy-start.8 = (s32[1024]{0:T(1024)S(1)}, s32[1024]{0:T(1024)}, u32[]{:S(2)}) copy-start(s32[1024]{0:T(1024)} %param.12) | copy-start | bytes 12292
  140.0 47.2 %all-to-all-start.1 = ((f32[162,8,128]{2,0,1:T(8,128)}), f32[162,8,128]{2,0,1:T(8,128)S(1)}, u32[]{:S(2)}, u32[]{:S(2)}) async-start(f32[162,8,128]{2,0,1:T(8,128)} %copy.31), calls=%async_computation.1 | async-start | bytes 1376256 | tf_op jit(solution)/shard_map/all_to_all | solution.py:86
  187.6 22.9 %copy-start.7 = (f32[128]{0:T(128)}, f32[128]{0:T(128)S(1)}, u32[]{:S(2)}) copy-start(f32[128]{0:T(128)S(1)} %get-tuple-element.3) | copy-start | bytes 1540
where the time goes:
time: 214 us; the launch traced here: 212 us
  other arithmetic  112 us (52%)
  local copies, waits for them, and re-layouts  62.7 us (29%)
  starting transfers between devices  17.4 us (8%)
  blocking collectives  15.6 us (7%)
  matrix products  2.4 us (1%)
    gather x2, local copies, waits for them, and re-layouts, per_device(): gathered_all = jnp.take(extended, neighbour.reshape(-1), axis=1)  39.8 us
    gather x31, other arithmetic, per_device(): dir_cosine[full_dir]  24.8 us
    gather x2, other arithmetic, per_device(): dir_sine[full_dir]  22.4 us
    gather x2, other arithmetic, per_device(): weight_col = band_weight[full_freq]  22.3 us
    div x1, other arithmetic, point_source(): relative = freq_col / top_freq  18 us
    all_to_all x1, blocking collectives, per_device(): lax.all_to_all(updated.reshape(comp_count * spec_count, 1, point_count),...  15.6 us
    all_to_all x1, starting transfers between devices, per_device(): lax.all_to_all(outgoing, 'space', split_axis=1, concat_axis=1, tiled=True)  12.2 us
    gather x1, local copies, waits for them, and re-layouts, per_device(): outgoing = jnp.take(masked, send_list[0].reshape(-1), axis=1)  6.64 us
  transfers between devices with their start and end apart: 2, of which 0 were waited for; matrix products, arithmetic and copies ran while one was open for 50% of the time, Pallas kernels for 0%

commit v1 on v0

--- a/solution.py
+++ b/solution.py
@@ -57,7 +57,9 @@
     wet_float = wet_mask.astype(jnp.float32)
     masked = spectra * wet_float[None, :]
     outgoing = jnp.take(masked, send_list[0].reshape(-1), axis=1)
-    ghost_values = lax.all_to_all(outgoing, "space", split_axis=1, concat_axis=1, tiled=True)
+    shards = jnp.split(outgoing, lax.axis_size("space"), axis=1)
+    got = lax.all_to_all(jnp.stack(shards), "space", 0, 0)
+    ghost_values = jnp.concatenate(got, axis=1)
     class_hits = (jnp.arange(NCLASS, dtype=jnp.int32)[:, None] == depth_class[None, :]).astype(
         jnp.float32
     )

time: 214 us -> 232 us (1.084)
  local copies, waits for them, and re-layouts: 62.7 us -> 83.4 us
    unnamed x23 -> x54, local copies, waits for them, and re-layouts: 2.64 us -> 22 us
  transfers between devices with their start and end apart: 2 -> 2, of which waited for: 0 -> 0; matrix products, arithmetic and copies ran while one was open for 50% -> 46% of each run, Pallas kernels for 0% -> 0%
where the time goes in v1:
time: 232 us; the launch traced here: 230 us
  other arithmetic  110 us (47%)
  local copies, waits for them, and re-layouts  83.4 us (36%)
  starting transfers between devices  17.5 us (8%)
  blocking collectives  15.6 us (7%)
  matrix products  2.4 us (1%)
    gather x2, local copies, waits for them, and re-layouts, per_device(): gathered_all = jnp.take(extended, neighbour.reshape(-1), axis=1)  39.8 us
    gather x31, other arithmetic, per_device(): dir_cosine[full_dir]  24.8 us
    gather x2, other arithmetic, per_device(): dir_sine[full_dir]  22.4 us
    gather x2, other arithmetic, per_device(): weight_col = band_weight[full_freq]  22.3 us
    unnamed x54, local copies, waits for them, and re-layouts  22 us
    div x1, other arithmetic, point_source(): relative = freq_col / top_freq  18 us
    all_to_all x1, blocking collectives, per_device(): lax.all_to_all(updated.reshape(comp_count * spec_count, 1, point_count),...  15.6 us
    all_to_all x1, starting transfers between devices, per_device(): got = lax.all_to_all(jnp.stack(shards), 'space', 0, 0)  12 us
  transfers between devices with their start and end apart: 2, of which 0 were waited for; matrix products, arithmetic and copies ran while one was open for 46% of the time, Pallas kernels for 0%

profile of v1, /device:TPU:1, one launch (start us, length us, event | category | flops | bytes accessed | tf_op | source)
XLA Modules:
  0.0 230.3 jit_solution(17810889938215656402)
XLA Ops:
  0.6 0.8 reshape_squeeze.6
  1.4 0.8 reshape_squeeze.5
  2.2 0.7 convert_element_type.4
  2.9 1.2 broadcast_multiply_fusion
  4.5 6.6 %gather_fusion.3 = f32[2048,162]{1,0:T(8,128)S(1)} fusion(f32[162,1024]{0,1:T(8,128)S(1)} %copy.29, s32[2048]{0:T(1024)S(1)} %broadcast_clamp_fusion.1), kind=kCustom, calls=%fused_computation.3 | custom fusion | bytes 2662400 | tf_op jit(solution)/shard_map/jit(_take)/gather | solution.py:59
  11.5 0.6 fusion.48
  12.1 0.6 fusion.47
  12.7 0.6 fusion.46
  13.3 0.6 fusion.45
  14.6 0.6 fusion.43
  15.2 0.6 fusion.42
  16.5 0.6 fusion.40
  17.1 0.6 fusion.39
  17.7 0.6 fusion.38
  19.6 0.6 fusion.35
  20.2 0.6 fusion.34
  20.8 0.6 fusion.33
  21.5 0.6 fusion.32
  22.7 0.6 fusion.30
  24.6 0.6 fusion.27
  25.2 0.6 fusion.26
  25.8 0.6 fusion.25
  26.4 0.6 fusion.24
  27.0 0.6 fusion.23
  28.3 0.6 fusion.21
  28.9 0.6 fusion.20
  29.5 0.6 fusion.19
  30.2 0.6 fusion.18
  30.8 0.6 fusion.17
  31.4 12.0 %all-to-all-start = ((f32[32,162,64]{1,2,0:T(8,128)}), f32[32,162,64]{1,2,0:T(8,128)S(1)}, u32[]{:S(2)}, u32[]{:S(2)}) async-start(f32[32,162,64]{1,2,0:T(8,128)} %fusion.17), calls=%async_computation | async-start | bytes 4194304 | tf_op jit(solution)/shard_map/all_to_all | solution.py:61
  43.6 0.6 fusion.59
  44.9 0.7 fusion.68
  45.7 0.7 fusion.67
  48.2 0.7 fusion.66
  48.9 0.7 fusion.65
  49.6 0.7 fusion.64
  50.4 0.7 fusion.63
  53.1 1.6 gather_fusion.2
  54.6 1.6 gather_fusion.1
  56.2 0.7 fusion.62
  57.1 0.7 gather_fusion
  57.8 0.8 dynamic-slice_cosine_fusion
  58.6 4.5 %fusion.50 = f32[1296]{0:T(1024)S(1)} fusion(f32[]{:T(128)} %bitcast.204, f32[]{:T(128)} %bitcast.205, f32[]{:T(128)} %bitcast.206, f32[]{:T(128)} %bitcast.207, f32[]{:T(128)} %bitcast.208, f32[]{:T(128)} %bitcast.210, f32[]{:T(128)} %bitcast.209), kind=kLoop, calls=%fused_computation.206 | loop fusion | flops 29808 | bytes 5212 | tf_op jit(solution)/shard_map/gather | solution.py:95
  63.1 4.3 %fusion.51 = f32[1296]{0:T(1024)S(1)} fusion(f32[]{:T(128)} %bitcast.95, f32[]{:T(128)} %bitcast.96, f32[]{:T(128)} %bitcast.97, f32[]{:T(128)} %bitcast.98, f32[]{:T(128)} %bitcast.99, f32[]{:T(128)} %bitcast.101, f32[]{:T(128)} %bitcast.100), kind=kLoop, calls=%fused_computation.207 | loop fusion | flops 29808 | bytes 5212 | tf_op jit(solution)/shard_map/gather | solution.py:94
  67.4 4.3 %fusion.52 = f32[1296]{0:T(1024)S(1)} fusion(f32[]{:T(128)} %bitcast.167, f32[]{:T(128)} %bitcast.168, f32[]{:T(128)} %bitcast.169, f32[]{:T(128)} %bitcast.170, f32[]{:T(128)} %bitcast.171, f32[]{:T(128)} %bitcast.173, f32[]{:T(128)} %bitcast.172), kind=kLoop, calls=%fused_computation.208 | loop fusion | flops 27216 | bytes 5212 | tf_op jit(solution)/shard_map/gather | solution.py:106
  71.8 17.8 %select_select_fusion = f32[1296]{0:T(1024)S(1)} fusion(pred[1296]{0:T(1024)(128)(4,1)S(1)} %compare_reduce_fusion.29, pred[1296]{0:T(1024)(128)(4,1)S(1)} %compare_reduce_fusion.30, pred[1296]{0:T(1024)(128)(4,1)S(1)} %compare_reduce_fusion.31, pred[1296]{0:T(1024)(128)(4,1)S(1)} %compare_reduce_fusion.32, pred[1296]{0:T(1024)(128)(4,1)S(1)} %compare_reduce_fusion.33, ...), kind=kLoop, calls=%fused_computation.199 | loop fusion | flops 37584 | bytes 48068 | tf_op jit(solution)/shard_map/gather | solution.py:95
  89.7 18.0 %broadcast_multiply_fusion.1 = (f32[1296]{0:T(1024)S(1)}, f32[1296]{0:T(1024)S(1)}) fusion(pred[1296]{0:T(1024)(128)(4,1)S(1)} %compare_reduce_fusion.29, pred[1296]{0:T(1024)(128)(4,1)S(1)} %compare_reduce_fusion.30, pred[1296]{0:T(1024)(128)(4,1)S(1)} %compare_reduce_fusion.31, pred[1296]{0:T(1024)(128)(4,1)S(1)} %compare_reduce_fusion.32, ...), kind=kLoop, calls=%fused_computation.213 | loop fusion | flops 38880 | bytes 53252 | tf_op jit(solution)/shard_map/div | solution.py:29
  107.7 1.0 slice_cosine_fusion.7
  108.7 1.3 copy-done.1
  110.0 2.1 pad_maximum_fusion
  112.1 31.4 %gather_fusion.4 = f32[8192,162]{1,0:T(8,128)} fusion(f32[162,3072]{0,1:T(8,128)S(1)} %pad_maximum_fusion, s32[8192]{0:T(1024)S(1)} %broadcast_clamp_fusion), kind=kCustom, calls=%fused_computation.4 | custom fusion | bytes 10649600 | tf_op jit(solution)/shard_map/jit(_take)/gather | solution.py:74
  143.5 8.4 %copy.30 = f32[8192,162]{0,1:T(8,128)} copy(f32[8192,162]{1,0:T(8,128)} %gather_fusion.4) | data formatting | bytes 10616832 | tf_op jit(solution)/shard_map/jit(_take)/gather | solution.py:74
  151.9 3.1 %select_bitcast_fusion = f32[162,8192]{1,0:T(8,128)S(1)} fusion(f32[8192,162]{0,1:T(8,128)} %copy.30, pred[8192]{0:T(1024)(128)(4,1)S(1)} %compare_and_fusion), kind=kLoop, calls=%fused_computation.5 | loop fusion | flops 1327104 | bytes 10625024 | tf_op jit(solution)/shard_map/jit(_take)/select_n | solution.py:74
  155.0 2.4 %fusion.3 = f32[162,1024]{1,0:T(8,128)S(1)} fusion(f32[162,8192]{1,0:T(8,128)S(1)} %select_bitcast_fusion, f32[162,32]{1,0:T(8,128)S(1)} %gather_fusion, f32[1024]{0:T(1024)S(1)} %bitcast.367, f32[1024]{0:T(1024)S(1)} %bitcast.373, f32[1024]{0:T(1024)S(1)} %bitcast.357, f32[1024]{0:T(1024)S(1)} %bitcast.366, f32[1024]{0:T(1024)S(1)} %bitcast.374, ...), kind=kOutput, calls=%fused_computation.12 | convolution fusion | flops 76009472 | bytes 6764048 | tf_op jit(solution)/shard_map/dot_general | solution.py:66
  157.6 1.0 copy.31
  158.6 5.4 %all-to-all-start.1 = ((f32[162,8,128]{2,0,1:T(8,128)}), f32[162,8,128]{2,0,1:T(8,128)S(1)}, u32[]{:S(2)}, u32[]{:S(2)}) async-start(f32[162,8,128]{2,0,1:T(8,128)} %copy.31), calls=%async_computation.1 | async-start | bytes 1376256 | tf_op jit(solution)/shard_map/all_to_all | solution.py:88
  164.2 4.6 %fusion.53 = f32[1296]{0:T(1024)S(1)} fusion(f32[]{:T(128)} %bitcast.131, f32[]{:T(128)} %bitcast.132, f32[]{:T(128)} %bitcast.133, f32[]{:T(128)} %bitcast.134, f32[]{:T(128)} %bitcast.135, f32[]{:T(128)} %bitcast.137, f32[]{:T(128)} %bitcast.136), kind=kLoop, calls=%fused_computation.209 | loop fusion | flops 27216 | bytes 5212 | tf_op jit(solution)/shard_map/gather | solution.py:105
  168.8 0.7 fusion.61
  169.5 18.1 %select_select_fusion.1 = f32[1296]{0:T(1024)S(1)} fusion(pred[1296]{0:T(1024)(128)(4,1)S(1)} %compare_reduce_fusion, pred[1296]{0:T(1024)(128)(4,1)S(1)} %compare_reduce_fusion.1, pred[1296]{0:T(1024)(128)(4,1)S(1)} %compare_reduce_fusion.2, pred[1296]{0:T(1024)(128)(4,1)S(1)} %compare_reduce_fusion.3, pred[1296]{0:T(1024)(128)(4,1)S(1)} %compare_reduce_fusion.4, ...), kind=kLoop, calls=%fused_computation.200 | loop fusion | flops 37584 | bytes 48068 | tf_op jit(solution)/shard_map/gather | solution.py:106
  187.6 18.2 %select_select_fusion.2 = f32[1296]{0:T(1024)S(1)} fusion(pred[1296]{0:T(1024)(128)(4,1)S(1)} %compare_reduce_fusion, pred[1296]{0:T(1024)(128)(4,1)S(1)} %compare_reduce_fusion.1, pred[1296]{0:T(1024)(128)(4,1)S(1)} %compare_reduce_fusion.2, pred[1296]{0:T(1024)(128)(4,1)S(1)} %compare_reduce_fusion.3, pred[1296]{0:T(1024)(128)(4,1)S(1)} %compare_reduce_fusion.4, ...), kind=kLoop, calls=%fused_computation.201 | loop fusion | flops 37584 | bytes 48068 | tf_op jit(solution)/shard_map/gather | solution.py:105
  206.4 1.1 exponential_multiply_fusion
  207.5 15.6 %all_to_all.35 = f32[1296,1,128]{2,1,0:T(1,128)S(1)} all-to-all(f32[1296,1,128]{2,1,0:T(1,128)S(1)} %bitcast.342), channel_id=1, replica_groups=mesh['space'=32,'spec'=8] {'spec'}, dimensions={0} | all-to-all | bytes 1327104 | tf_op jit(solution)/shard_map/all_to_all | solution.py:110
  223.6 5.5 %reduce.129 = f32[1296,128]{1,0:T(8,128)S(1)} reduce(f32[1296,1,128]{2,1,0:T(1,128)S(1)} %all_to_all.35, f32[]{:T(128)} %broadcast.1222), dimensions={1}, to_apply=%all_to_all.29.reduce_sub_computation.3 | reduce | bytes 1327108 | tf_op jit(solution)/shard_map/all_to_all | solution.py:110
  229.4 1.0 copy.40
  (115 shorter events, 11.4 us)
Async XLA Ops:
  4.4 6.7 %copy-start = (f32[162,1024]{0,1:T(8,128)}, f32[162,1024]{0,1:T(8,128)S(1)}, u32[]{:S(2)}) copy-start(f32[162,1024]{0,1:T(8,128)S(1)} %copy.29) | copy-start | bytes 1990660
  31.4 77.3 %all-to-all-start = ((f32[32,162,64]{1,2,0:T(8,128)}), f32[32,162,64]{1,2,0:T(8,128)S(1)}, u32[]{:S(2)}, u32[]{:S(2)}) async-start(f32[32,162,64]{1,2,0:T(8,128)} %fusion.17), calls=%async_computation | async-start | bytes 4194304 | tf_op jit(solution)/shard_map/all_to_all | solution.py:61
  43.5 13.5 %copy-start.3 = (s32[8,1024]{1,0:T(8,128)S(1)}, s32[8,1024]{1,0:T(8,128)}, u32[]{:S(2)}) copy-start(s32[8,1024]{1,0:T(8,128)} %param.14) | copy-start | bytes 98308
  43.5 13.5 %copy-start.6 = (f32[36,32]{0,1:T(8,128)S(1)}, f32[36,32]{0,1:T(8,128)}, u32[]{:S(2)}) copy-start(f32[36,32]{0,1:T(8,128)} %param.13) | copy-start | bytes 13828
  43.5 28.3 %copy-start.5 = (f32[8,1024]{1,0:T(8,128)S(1)}, f32[8,1024]{1,0:T(8,128)}, u32[]{:S(2)}) copy-start(f32[8,1024]{1,0:T(8,128)} %param.15) | copy-start | bytes 98308
  43.5 64.2 %copy-start.4 = (f32[8,1024]{1,0:T(8,128)S(1)}, f32[8,1024]{1,0:T(8,128)}, u32[]{:S(2)}) copy-start(f32[8,1024]{1,0:T(8,128)} %param.16) | copy-start | bytes 98308
  108.7 1.4 copy-start.1
  151.9 3.1 %copy-start.2 = (f32[162,1024]{1,0:T(8,128)S(1)}, f32[162,1024]{1,0:T(8,128)}, u32[]{:S(2)}) copy-start(f32[162,1024]{1,0:T(8,128)} %param.10) | copy-start | bytes 1990660
  151.9 3.1 %copy-start.8 = (s32[1024]{0:T(1024)S(1)}, s32[1024]{0:T(1024)}, u32[]{:S(2)}) copy-start(s32[1024]{0:T(1024)} %param.12) | copy-start | bytes 12292
  158.6 47.3 %all-to-all-start.1 = ((f32[162,8,128]{2,0,1:T(8,128)}), f32[162,8,128]{2,0,1:T(8,128)S(1)}, u32[]{:S(2)}, u32[]{:S(2)}) async-start(f32[162,8,128]{2,0,1:T(8,128)} %copy.31), calls=%async_computation.1 | async-start | bytes 1376256 | tf_op jit(solution)/shard_map/all_to_all | solution.py:88
  206.4 22.8 %copy-start.7 = (f32[128]{0:T(128)}, f32[128]{0:T(128)S(1)}, u32[]{:S(2)}) copy-start(f32[128]{0:T(128)S(1)} %get-tuple-element.3) | copy-start | bytes 1540
